TPU v7x, 32 devices: a whole 2x2x4 slice. The times are simulated.
32 devices in a mesh: groups: 2 (over y), tile: 4 (over z), sub: 2 (over x), rep: 2 (over core).
Axes of the slice: x: 2, y: 2, z: 4, core: 2. Of those that a mesh axis runs over, the one named last changes fastest.
Arguments:
- pressure: float32 [64, 32, 256], P(('groups', 'tile'), 'sub', 'rep'), parts along dimension 0, may hold values from -3 to 3
- previous_pressure: float32 [64, 32, 256], P(('groups', 'tile'), 'sub', 'rep'), parts along dimension 0, may hold values from -3 to 3
- courant_square: float32 [64, 32, 256], P(('groups', 'tile'), 'sub', 'rep'), parts along dimension 0, may hold values from 0.07 to 0.22
- node_area: float32 [12288], P(('groups', 'tile', 'sub', 'rep')), parts along dimension 0, may hold values from 0.25 to 4
- mode_shapes: bfloat16 [12288, 2048], P(('groups', 'tile', 'sub', 'rep')), parts along dimension 0, may hold values from -0.049804688 to 0.049804688
- frequency: float32 [4096], P('groups'), parts along dimension 0, may hold values from 0.4 to 1.3
- damping_ratio: float32 [4096], P('groups'), parts along dimension 0, may hold values from 0.02 to 0.4
- modal_start: float32 [2, 4096], P(None, 'groups'), parts along dimension 1, may hold values from -4 to 4
- slot_cell: int32 [8, 2, 2, 384], P(('groups', 'tile'), 'sub', 'rep'), parts along dimension 0, may hold values from 0 to 16383, as said below
- slot_owner: int32 [8, 2, 2, 384, 1], P(('groups', 'tile'), 'sub', 'rep'), parts along dimension 0, may hold values from 0 to 3; in each aligned block of 384 rows (0 to 383, 384 to 767, ..., all dimensions but the last counted through in order) at most 96 rows name the same one
- surface_count: int32 [4, 2, 4], P(('groups', 'sub'), 'rep', 'tile'), parts along dimension 0, may hold values from 1 to 384, 512 in all within a row
Outputs:
- final_pressure: float32 [64, 32, 256], P(('groups', 'tile'), 'sub', 'rep'), parts along dimension 0
- prior_pressure: float32 [64, 32, 256], P(('groups', 'tile'), 'sub', 'rep'), parts along dimension 0
- surface_accel: bfloat16 [8, 2, 2, 4, 384], P(('groups', 'tile'), 'sub', 'rep'), parts along dimension 0
- modal_state: float32 [2, 4096], P(None, ('groups', 'tile', 'sub', 'rep')), parts along dimension 1
There are 2 independent parts, one for each index of `groups`. A program takes and returns all parts, laid end to end along the dimension named above; each array names one. Nothing has to cross between parts.
Inputs may be any that keep to these rules, and one draw needn't show every extreme that they name: `slot_cell`: slot j of a block lies in the block's cells j * (42) to (j + 1) (42) - 1, so a block's slots name distinct cells. `slot_owner`: every owner index is named by exactly 96 of the 384 slots of each block (t, s, r). `surface_count`: for fixed s and r the counts over t sum to 128 times the number of tile indices, and one of them equals 384.
All inputs are finite; a program needn't handle non-finite values. No bound on the sum of `surface_count` on one device may be relied on, other than what follows from the above.
Results may differ from a plain program's by a relative error of at most 0.0098.
Values may be sent and summed in bfloat16 or wider, within the bound.
A program may use at most 64 MiB of HBM per device.

v0:
```python
import jax
import jax.numpy as jnp
from jax import lax
from jax.sharding import PartitionSpec as P

STEPS = 4
HALO = 4
nonlinear = 0.03
viscous = 0.02


def extended(shard, sides, width):
    for axis, dim in sides:
        count, length = (lax.axis_size(axis), shard.shape[dim])
        up = [(i, (i + 1) % count) for i in range(count - 1)]
        down = [(j, i) for i, j in up]
        last = lax.slice_in_dim(shard, length - width, length, axis=dim)
        first = lax.slice_in_dim(shard, 0, width, axis=dim)
        before = lax.ppermute(last, axis, up)
        after = lax.ppermute(first, axis, down)
        shard = jnp.concatenate([before, shard, after], axis=dim)
    return shard


def laplace(padded):
    middle = padded[1:-1, 1:-1, 1:-1]
    summed = padded[2:, 1:-1, 1:-1] + padded[:-2, 1:-1, 1:-1]
    summed = summed + padded[1:-1, 2:, 1:-1] + padded[1:-1, :-2, 1:-1]
    summed = summed + padded[1:-1, 1:-1, 2:] + padded[1:-1, 1:-1, :-2]
    return summed - 6.0 * middle


def advance(wide_now, wide_before, coefficient):
    current = wide_now[1:-1, 1:-1, 1:-1]
    before = wide_before[1:-1, 1:-1, 1:-1]
    change = current - before
    driving = (
        coefficient * laplace(wide_now)
        + viscous * laplace(wide_now - wide_before)
        + 2.0 * nonlinear * change * change
    )
    return 2.0 * current - before + (1.0 + 2.0 * nonlinear * current) * driving


def routing(owners, live_count, tile_total):
    slot_total = owners.shape[0]
    bucket = slot_total // tile_total
    position = jnp.arange(slot_total, dtype=jnp.int32)
    is_live = position < live_count
    member = (
        (owners[:, None] == jnp.arange(tile_total, dtype=jnp.int32)[None, :]) & is_live[:, None]
    ).astype(jnp.float32)
    earlier = (position[None, :] < position[:, None]).astype(jnp.float32)
    before = jnp.dot(earlier, member, precision=lax.Precision.HIGHEST)
    bucket_rank = jnp.sum(before * member, axis=1).astype(jnp.int32)
    target = owners * bucket + bucket_rank
    return ((target[:, None] == position[None, :]) & is_live[:, None]).astype(jnp.bfloat16)


def oscillate(forces, frequency, damping_ratio, start_state):

    def advance_mode(carried, force_row):
        displace, velocity = carried
        acceleration = (
            force_row
            - 2.0 * damping_ratio * frequency * velocity
            - frequency * frequency * displace
        )
        velocity = velocity + acceleration
        displace = displace + velocity
        return ((displace, velocity), acceleration)

    (displace, velocity), modal_accel = lax.scan(
        advance_mode, (start_state[0], start_state[1]), forces
    )
    return (modal_accel, jnp.stack([displace, velocity]))


def trim_rim(array, depth):
    return array[
        depth : array.shape[0] - depth,
        depth : array.shape[1] - depth,
        depth : array.shape[2] - depth,
    ]


def inside_range(offset, length, axis_devices, margin):
    position = offset * length - margin + jnp.arange(length + 2 * margin, dtype=jnp.int32)
    return ((position >= 0) & (position < axis_devices * length)).astype(jnp.float32)


def body(
    pressure,
    previous_pressure,
    courant_square,
    node_area,
    mode_shapes,
    frequency,
    damping_ratio,
    modal_start,
    slot_cell,
    slot_owner,
    surface_count,
):
    tile_total = lax.axis_size("tile")
    extent_first, extent_second, extent_third = pressure.shape
    slot_total = slot_cell.shape[-1]
    bucket = slot_total // tile_total
    routing_matrix = routing(slot_owner.reshape(slot_total), surface_count.reshape(()), tile_total)
    cell_index = slot_cell.reshape(slot_total)
    fields = jnp.stack([pressure, previous_pressure])
    margin = HALO
    coef_wide = extended(courant_square, (("tile", 0), ("sub", 1), ("rep", 2)), margin)
    inside_first = inside_range(lax.axis_index("tile"), extent_first, lax.axis_size("tile"), margin)
    inside_second = inside_range(lax.axis_index("sub"), extent_second, lax.axis_size("sub"), margin)
    inside_third = inside_range(lax.axis_index("rep"), extent_third, lax.axis_size("rep"), margin)
    inside = (
        inside_first[:, None, None] * inside_second[None, :, None] * inside_third[None, None, :]
    )

    def deep_block(carried, unused):
        padded = extended(carried, (("tile", 1), ("sub", 2), ("rep", 3)), margin)
        recorded = []
        for layer_index in range(margin):
            edge_depth = layer_index + 1
            updated = advance(padded[0], padded[1], trim_rim(coef_wide, edge_depth)) * trim_rim(
                inside, edge_depth
            )
            interior = trim_rim(updated, margin - edge_depth)
            recorded.append(jnp.take(interior.reshape(-1), cell_index).astype(jnp.bfloat16))
            padded = jnp.stack([updated, trim_rim(padded[0], 1)])
        return (padded, jnp.stack(recorded))

    fields, history = lax.scan(deep_block, fields, None, length=STEPS // margin)
    history = history.reshape(STEPS, slot_total)
    final_field = fields[0]
    prior_field = fields[1]
    bucketed = jnp.dot(history, routing_matrix, preferred_element_type=jnp.float32).astype(
        jnp.bfloat16
    )
    bucketed = bucketed.reshape(STEPS, tile_total, bucket)
    arrived = lax.all_to_all(bucketed, "tile", split_axis=1, concat_axis=1, tiled=True)
    arrived_flat = arrived.reshape(arrived.shape[0], slot_total)
    weighted = (arrived_flat * node_area).astype(jnp.bfloat16)
    partial_forces = jnp.dot(weighted, mode_shapes, preferred_element_type=jnp.float32)
    device_total = lax.axis_size("tile") * lax.axis_size("sub") * lax.axis_size("rep")
    mode_count = mode_shapes.shape[1]
    mode_share = mode_count // device_total
    first_mode = lax.axis_index(("tile", "sub", "rep")) * mode_share
    forces = lax.psum_scatter(
        partial_forces, ("tile", "sub", "rep"), scatter_dimension=1, tiled=True
    )
    local_frequency = lax.dynamic_slice_in_dim(frequency, first_mode, mode_share, 0)
    local_damping = lax.dynamic_slice_in_dim(damping_ratio, first_mode, mode_share, 0)
    local_start = lax.dynamic_slice_in_dim(modal_start, first_mode, mode_share, 1)
    modal_accel, modal_state = oscillate(forces, local_frequency, local_damping, local_start)
    modal_rounded = modal_accel.astype(jnp.bfloat16)
    node_accel = lax.dot_general(
        lax.all_gather(modal_rounded, ("tile", "sub", "rep"), axis=1, tiled=True),
        mode_shapes,
        (((1,), (1,)), ((), ())),
        preferred_element_type=jnp.float32,
    )
    outgoing = node_accel.astype(jnp.bfloat16).reshape(STEPS, tile_total, bucket)
    returned = lax.all_to_all(outgoing, "tile", split_axis=1, concat_axis=1, tiled=True)
    surface = lax.dot_general(
        returned.reshape(STEPS, slot_total),
        routing_matrix,
        (((1,), (1,)), ((), ())),
        preferred_element_type=jnp.float32,
    )
    surface_accel = surface.astype(jnp.bfloat16).reshape(1, 1, 1, STEPS, slot_total)
    return (final_field, prior_field, surface_accel, modal_state)


def solution(mesh):
    in_specs = (
        P(("groups", "tile"), "sub", "rep"),
        P(("groups", "tile"), "sub", "rep"),
        P(("groups", "tile"), "sub", "rep"),
        P(("groups", "tile", "sub", "rep")),
        P(("groups", "tile", "sub", "rep"), None),
        P("groups"),
        P("groups"),
        P(None, "groups"),
        P(("groups", "tile"), "sub", "rep", None),
        P(("groups", "tile"), "sub", "rep", None, None),
        P(("groups", "sub"), "rep", "tile"),
    )
    out_specs = (
        P(("groups", "tile"), "sub", "rep"),
        P(("groups", "tile"), "sub", "rep"),
        P(("groups", "tile"), "sub", "rep", None, None),
        P(None, ("groups", "tile", "sub", "rep")),
    )
    return jax.shard_map(body, mesh=mesh, in_specs=in_specs, out_specs=out_specs, check_vma=False)
```

profile of v0, /device:TPU:0, one launch (start us, length us, event | category | flops | bytes accessed | tf_op | source)
XLA Modules:
  0.0 172.1 jit_solution(446253793117891918)
XLA Ops:
  7.2 0.9 fusion.41
  8.1 5.0 %collective-permute-start = (f32[2,4,16,128]{3,2,1,0:T(8,128)S(1)}, f32[2,4,16,128]{3,2,1,0:T(8,128)S(1)}, u32[]{:S(2)}, u32[]{:S(2)}) collective-permute-start(f32[2,4,16,128]{3,2,1,0:T(8,128)S(1)} %get-tuple-element.142), channel_id=1, source_target_pairs={{0,4},{4,8},{8,12},{1,5},{5,9},{9,13},{2,6},{6,10},{10,14},{3,7},{... | collective-permute-start | bytes 196616 | tf_op jit(solution)/shard_map/while/body/eval_jaxpr/ppermute | solution.py:19
  13.1 1.3 collective-permute-start.1
  14.4 0.8 fusion.70
  15.2 4.5 %collective-permute-start.6 = (f32[4,16,128]{2,1,0:T(8,128)S(1)}, f32[4,16,128]{2,1,0:T(8,128)S(1)}, u32[]{:S(2)}, u32[]{:S(2)}) collective-permute-start(f32[4,16,128]{2,1,0:T(8,128)S(1)} %get-tuple-element.145), channel_id=1, source_target_pairs={{0,4},{4,8},{8,12},{1,5},{5,9},{9,13},{2,6},{6,10},{10,14},{3,7},{... | collective-permute-start | bytes 98312 | tf_op jit(solution)/shard_map/ppermute | solution.py:19
  19.7 1.3 collective-permute-start.7
  21.1 0.7 reduce
  22.5 0.7 reduce.1
  23.2 0.2 fusion.1
  23.4 0.1 broadcast_multiply_fusion.1
  23.5 0.1 broadcast_multiply_fusion
  23.6 0.7 constant_dynamic-slice_fusion
  24.3 0.8 constant_dynamic-update-slice_fusion.1
  25.1 0.4 collective-permute-done.7
  25.6 3.4 %collective-permute-start.8 = (f32[16,4,128]{2,1,0:T(4,128)S(1)}, f32[16,4,128]{2,1,0:T(4,128)S(1)}, u32[]{:S(2)}, u32[]{:S(2)}) collective-permute-start(f32[16,4,128]{2,1,0:T(4,128)S(1)} %get-tuple-element.140), channel_id=1, source_target_pairs={{0,2},{1,3},{4,6},{5,7},{8,10},{9,11},{12,14},{13,15},{16,18},{17,... | collective-permute-start | bytes 98312 | tf_op jit(solution)/shard_map/ppermute | solution.py:19
  29.0 1.3 collective-permute-start.9
  30.3 0.8 pad_maximum_fusion.7
  31.1 4.5 %collective-permute-start.2 = (f32[2,16,4,128]{3,2,1,0:T(4,128)S(1)}, f32[2,16,4,128]{3,2,1,0:T(4,128)S(1)}, u32[]{:S(2)}, u32[]{:S(2)}) collective-permute-start(f32[2,16,4,128]{3,2,1,0:T(4,128)S(1)} %get-tuple-element.136), channel_id=1, source_target_pairs={{0,2},{1,3},{4,6},{5,7},{8,10},{9,11},{12,14},{13,15},{16,18},{17,... | collective-permute-start | bytes 196616 | tf_op jit(solution)/shard_map/while/body/eval_jaxpr/ppermute | solution.py:19
  35.7 1.3 collective-permute-start.3
  37.1 0.1 fusion.68
  37.2 1.3 collective-permute-start.10
  38.5 1.3 collective-permute-start.11
  39.8 2.1 %collective-permute-done.3 = f32[2,16,4,128]{3,2,1,0:T(4,128)S(1)} collective-permute-done((f32[2,16,4,128]{3,2,1,0:T(4,128)S(1)}, f32[2,16,4,128]{3,2,1,0:T(4,128)S(1)}, u32[]{:S(2)}, u32[]{:S(2)}) %collective-permute-start.3) | collective-permute-done | bytes 65568 | tf_op jit(solution)/shard_map/while/body/eval_jaxpr/ppermute | solution.py:20
  41.9 0.1 pad_maximum_fusion.1
  41.9 0.2 fusion.67
  42.1 1.3 collective-permute-start.4
  43.4 1.3 collective-permute-start.5
  44.7 0.3 pad_maximum_fusion.2
  45.1 2.0 %collective-permute-done.5 = f32[2,16,24,4]{3,2,1,0:T(8,128)S(1)} collective-permute-done((f32[2,16,24,4]{3,2,1,0:T(8,128)S(1)}, f32[2,16,24,4]{3,2,1,0:T(8,128)S(1)}, u32[]{:S(2)}, u32[]{:S(2)}) %collective-permute-start.5) | collective-permute-done | bytes 12320 | tf_op jit(solution)/shard_map/while/body/eval_jaxpr/ppermute | solution.py:20
  47.0 0.5 pad_maximum_fusion
  47.6 0.1 slice_bitcast_fusion
  47.6 0.1 fusion.60
  47.7 1.4 slice_subtract_fusion
  49.1 0.1 slice.514
  49.2 1.2 slice_subtract_fusion.1
  50.4 0.1 slice.499
  50.5 1.0 slice_subtract_fusion.2
  51.6 0.3 fusion.40
  51.9 2.5 %gather_fusion.2 = bf16[384]{0:T(512)(128)(2,1)S(1)} fusion(f32[16384]{0:T(1024)S(1)} %bitcast.42, s32[1024]{0:T(1024)S(1)} %pad_clamp_fusion), kind=kCustom, calls=%fused_computation.2.clone | custom fusion | bytes 3072 | tf_op jit(solution)/shard_map/while/body/eval_jaxpr/jit(_take)/gather | solution.py:130
  54.5 2.5 %gather_fusion.3 = bf16[384]{0:T(512)(128)(2,1)S(1)} fusion(f32[16384]{0:T(1024)S(1)} %bitcast.41, s32[1024]{0:T(1024)S(1)} %pad_clamp_fusion), kind=kCustom, calls=%fused_computation.3.clone | custom fusion | bytes 3072 | tf_op jit(solution)/shard_map/while/body/eval_jaxpr/jit(_take)/gather | solution.py:130
  57.0 2.8 %gather_fusion.1 = bf16[384]{0:T(512)(128)(2,1)S(1)} fusion(bf16[16384]{0:T(1024)(128)(2,1)S(1)} %bitcast.40, s32[1024]{0:T(1024)S(1)} %pad_clamp_fusion), kind=kCustom, calls=%fused_computation.1.clone | custom fusion | bytes 3072 | tf_op jit(solution)/shard_map/while/body/eval_jaxpr/jit(_take)/gather | solution.py:130
  59.9 2.8 %gather_fusion = bf16[384]{0:T(512)(128)(2,1)S(1)} fusion(bf16[16384]{0:T(1024)(128)(2,1)S(1)} %bitcast.39, s32[1024]{0:T(1024)S(1)} %pad_clamp_fusion), kind=kCustom, calls=%fused_computation.clone | custom fusion | bytes 3072 | tf_op jit(solution)/shard_map/while/body/eval_jaxpr/jit(_take)/gather | solution.py:130
  62.8 0.3 convolution_convert_fusion.1
  63.1 0.1 reshape.135
  63.1 0.6 copy.17
  63.7 5.5 %all-to-all-start = ((bf16[4,4,96]{2,0,1:T(4,128)(2,1)}), bf16[4,4,96]{2,0,1:T(4,128)(2,1)S(1)}, u32[]{:S(2)}, u32[]{:S(2)}) async-start(bf16[4,4,96]{2,0,1:T(4,128)(2,1)} %copy.17), calls=%async_computation | async-start | bytes 8192 | tf_op jit(solution)/shard_map/all_to_all | solution.py:142
  69.3 5.6 %all-to-all-done = bf16[4,4,96]{2,0,1:T(4,128)(2,1)S(1)} async-done(((bf16[4,4,96]{2,0,1:T(4,128)(2,1)}), bf16[4,4,96]{2,0,1:T(4,128)(2,1)S(1)}, u32[]{:S(2)}, u32[]{:S(2)}) %all-to-all-start) | async-done | bytes 3104 | tf_op jit(solution)/shard_map/all_to_all | solution.py:142
  74.9 0.1 reshape.139
  75.0 1.7 %convolution_bitcast_fusion = f32[2048,4]{1,0:T(8,128)} fusion(bf16[384,2048]{1,0:T(8,128)(2,1)S(1)} %copy-done, f32[4,384]{1,0:T(4,128)S(1)} %reshape.139, f32[384]{0:T(512)S(1)} %copy-done.6), kind=kOutput, calls=%fused_computation.6 | convolution fusion | flops 6294528 | bytes 1613312
  76.7 0.0 reduce-scatter.4.cloned.1.call-update
  76.7 0.8 fusion.63
  77.5 0.8 dynamic_slice.15
  78.3 55.4 %reduce-scatter.4.cloned.1.call-done = f32[128,4]{1,0:T(8,128)} async-done(((f32[2048,4]{1,0:T(8,128)}), f32[128,4]{1,0:T(8,128)}) %reduce-scatter.4.cloned.1.call-update) | async-done | bytes 2064
  133.7 0.9 copy.22
  134.6 0.3 while.4
  134.9 19.4 %all_gather.3 = bf16[4,2048]{1,0:T(4,128)(2,1)S(1)} all-gather(bf16[4,128]{1,0:T(4,128)(2,1)S(1)} %get-tuple-element.98), channel_id=1, replica_groups=mesh['groups'=2,'tile'=4,'sub'=2,'rep'=2] {'tile','sub','rep'}, dimensions={1}, use_global_device_ids=true | all-gather | bytes 17408 | tf_op jit(solution)/shard_map/all_gather | solution.py:159
  154.2 0.5 convolution_convert_fusion.2
  154.8 0.1 reshape.136
  154.8 0.6 copy.19
  155.5 3.2 %all-to-all-start.1 = ((bf16[4,4,96]{2,0,1:T(4,128)(2,1)}), bf16[4,4,96]{2,0,1:T(4,128)(2,1)S(1)}, u32[]{:S(2)}, u32[]{:S(2)}) async-start(bf16[4,4,96]{2,0,1:T(4,128)(2,1)} %copy.19), calls=%async_computation.1 | async-start | bytes 8192 | tf_op jit(solution)/shard_map/all_to_all | solution.py:165
  158.7 0.6 pad_maximum_fusion.9
  159.3 5.0 %all-to-all-done.1 = bf16[4,4,96]{2,0,1:T(4,128)(2,1)S(1)} async-done(((bf16[4,4,96]{2,0,1:T(4,128)(2,1)}), bf16[4,4,96]{2,0,1:T(4,128)(2,1)S(1)}, u32[]{:S(2)}, u32[]{:S(2)}) %all-to-all-start.1) | async-done | bytes 3104 | tf_op jit(solution)/shard_map/all_to_all | solution.py:165
  164.3 0.1 reshape.137
  164.4 0.9 fusion.2
  (53 shorter events, 0.5 us)
Async XLA Ops:
  7.2 67.8 %copy-start = (bf16[384,2048]{1,0:T(8,128)(2,1)S(1)}, bf16[384,2048]{1,0:T(8,128)(2,1)}, u32[]{:S(2)}) copy-start(bf16[384,2048]{1,0:T(8,128)(2,1)} %param.19) | copy-start | bytes 4718596
  7.2 34.7 %copy-start.3 = (f32[8,16,128]{2,1,0:T(8,128)S(1)}, f32[8,16,128]{2,1,0:T(8,128)}, u32[]{:S(2)}) copy-start(f32[8,16,128]{2,1,0:T(8,128)} %param.15) | copy-start | bytes 196612
  7.2 34.7 %copy-start.4 = (f32[8,16,128]{2,1,0:T(8,128)S(1)}, f32[8,16,128]{2,1,0:T(8,128)}, u32[]{:S(2)}) copy-start(f32[8,16,128]{2,1,0:T(8,128)} %param.16) | copy-start | bytes 196612
  8.1 22.1 %collective-permute-start = (f32[2,4,16,128]{3,2,1,0:T(8,128)S(1)}, f32[2,4,16,128]{3,2,1,0:T(8,128)S(1)}, u32[]{:S(2)}, u32[]{:S(2)}) collective-permute-start(f32[2,4,16,128]{3,2,1,0:T(8,128)S(1)} %get-tuple-element.142), channel_id=1, source_target_pairs={{0,4},{4,8},{8,12},{1,5},{5,9},{9,13},{2,6},{6,10},{10,14},{3,7},{... | collective-permute-start | bytes 196616 | tf_op jit(solution)/shard_map/while/body/eval_jaxpr/ppermute | solution.py:19
  13.1 17.2 %collective-permute-start.1 = (f32[2,4,16,128]{3,2,1,0:T(8,128)S(1)}, f32[2,4,16,128]{3,2,1,0:T(8,128)S(1)}, u32[]{:S(2)}, u32[]{:S(2)}) collective-permute-start(f32[2,4,16,128]{3,2,1,0:T(8,128)S(1)} %get-tuple-element.143), channel_id=1, source_target_pairs={{4,0},{8,4},{12,8},{5,1},{9,5},{13,9},{6,2},{10,6},{14,10},{7,3},{... | collective-permute-start | bytes 196616 | tf_op jit(solution)/shard_map/while/body/eval_jaxpr/ppermute | solution.py:20
  15.2 9.1 %collective-permute-start.6 = (f32[4,16,128]{2,1,0:T(8,128)S(1)}, f32[4,16,128]{2,1,0:T(8,128)S(1)}, u32[]{:S(2)}, u32[]{:S(2)}) collective-permute-start(f32[4,16,128]{2,1,0:T(8,128)S(1)} %get-tuple-element.145), channel_id=1, source_target_pairs={{0,4},{4,8},{8,12},{1,5},{5,9},{9,13},{2,6},{6,10},{10,14},{3,7},{... | collective-permute-start | bytes 98312 | tf_op jit(solution)/shard_map/ppermute | solution.py:19
  19.7 5.8 %collective-permute-start.7 = (f32[4,16,128]{2,1,0:T(8,128)S(1)}, f32[4,16,128]{2,1,0:T(8,128)S(1)}, u32[]{:S(2)}, u32[]{:S(2)}) collective-permute-start(f32[4,16,128]{2,1,0:T(8,128)S(1)} %get-tuple-element.144), channel_id=1, source_target_pairs={{4,0},{8,4},{12,8},{5,1},{9,5},{13,9},{6,2},{10,6},{14,10},{7,3},{... | collective-permute-start | bytes 98312 | tf_op jit(solution)/shard_map/ppermute | solution.py:20
  25.6 11.4 %collective-permute-start.8 = (f32[16,4,128]{2,1,0:T(4,128)S(1)}, f32[16,4,128]{2,1,0:T(4,128)S(1)}, u32[]{:S(2)}, u32[]{:S(2)}) collective-permute-start(f32[16,4,128]{2,1,0:T(4,128)S(1)} %get-tuple-element.140), channel_id=1, source_target_pairs={{0,2},{1,3},{4,6},{5,7},{8,10},{9,11},{12,14},{13,15},{16,18},{17,... | collective-permute-start | bytes 98312 | tf_op jit(solution)/shard_map/ppermute | solution.py:19
  29.0 8.0 %collective-permute-start.9 = (f32[16,4,128]{2,1,0:T(4,128)S(1)}, f32[16,4,128]{2,1,0:T(4,128)S(1)}, u32[]{:S(2)}, u32[]{:S(2)}) collective-permute-start(f32[16,4,128]{2,1,0:T(4,128)S(1)} %get-tuple-element.141), channel_id=1, source_target_pairs={{2,0},{3,1},{6,4},{7,5},{10,8},{11,9},{14,12},{15,13},{18,16},{19,... | collective-permute-start | bytes 98312 | tf_op jit(solution)/shard_map/ppermute | solution.py:20
  31.1 8.6 %collective-permute-start.2 = (f32[2,16,4,128]{3,2,1,0:T(4,128)S(1)}, f32[2,16,4,128]{3,2,1,0:T(4,128)S(1)}, u32[]{:S(2)}, u32[]{:S(2)}) collective-permute-start(f32[2,16,4,128]{3,2,1,0:T(4,128)S(1)} %get-tuple-element.136), channel_id=1, source_target_pairs={{0,2},{1,3},{4,6},{5,7},{8,10},{9,11},{12,14},{13,15},{16,18},{17,... | collective-permute-start | bytes 196616 | tf_op jit(solution)/shard_map/while/body/eval_jaxpr/ppermute | solution.py:19
  35.7 6.2 %collective-permute-start.3 = (f32[2,16,4,128]{3,2,1,0:T(4,128)S(1)}, f32[2,16,4,128]{3,2,1,0:T(4,128)S(1)}, u32[]{:S(2)}, u32[]{:S(2)}) collective-permute-start(f32[2,16,4,128]{3,2,1,0:T(4,128)S(1)} %get-tuple-element.137), channel_id=1, source_target_pairs={{2,0},{3,1},{6,4},{7,5},{10,8},{11,9},{14,12},{15,13},{18,16},{19,... | collective-permute-start | bytes 196616 | tf_op jit(solution)/shard_map/while/body/eval_jaxpr/ppermute | solution.py:20
  37.2 7.6 %collective-permute-start.10 = (f32[16,24,4]{2,1,0:T(8,128)S(1)}, f32[16,24,4]{2,1,0:T(8,128)S(1)}, u32[]{:S(2)}, u32[]{:S(2)}) collective-permute-start(f32[16,24,4]{2,1,0:T(8,128)S(1)} %get-tuple-element.138), channel_id=1, source_target_pairs={{0,1},{2,3},{4,5},{6,7},{8,9},{10,11},{12,13},{14,15},{16,17},{18,... | collective-permute-start | bytes 18440 | tf_op jit(solution)/shard_map/ppermute | solution.py:19
  38.5 6.3 %collective-permute-start.11 = (f32[16,24,4]{2,1,0:T(8,128)S(1)}, f32[16,24,4]{2,1,0:T(8,128)S(1)}, u32[]{:S(2)}, u32[]{:S(2)}) collective-permute-start(f32[16,24,4]{2,1,0:T(8,128)S(1)} %get-tuple-element.139), channel_id=1, source_target_pairs={{1,0},{3,2},{5,4},{7,6},{9,8},{11,10},{13,12},{15,14},{17,16},{19,... | collective-permute-start | bytes 18440 | tf_op jit(solution)/shard_map/ppermute | solution.py:20
  42.1 2.9 %collective-permute-start.4 = (f32[2,16,24,4]{3,2,1,0:T(8,128)S(1)}, f32[2,16,24,4]{3,2,1,0:T(8,128)S(1)}, u32[]{:S(2)}, u32[]{:S(2)}) collective-permute-start(f32[2,16,24,4]{3,2,1,0:T(8,128)S(1)} %get-tuple-element.134), channel_id=1, source_target_pairs={{0,1},{2,3},{4,5},{6,7},{8,9},{10,11},{12,13},{14,15},{16,17},{18,... | collective-permute-start | bytes 36872 | tf_op jit(solution)/shard_map/while/body/eval_jaxpr/ppermute | solution.py:19
  43.4 3.6 %collective-permute-start.5 = (f32[2,16,24,4]{3,2,1,0:T(8,128)S(1)}, f32[2,16,24,4]{3,2,1,0:T(8,128)S(1)}, u32[]{:S(2)}, u32[]{:S(2)}) collective-permute-start(f32[2,16,24,4]{3,2,1,0:T(8,128)S(1)} %get-tuple-element.135), channel_id=1, source_target_pairs={{1,0},{3,2},{5,4},{7,6},{9,8},{11,10},{13,12},{15,14},{17,16},{19,... | collective-permute-start | bytes 36872 | tf_op jit(solution)/shard_map/while/body/eval_jaxpr/ppermute | solution.py:20
  50.5 1.1 copy-start.5
  51.9 7.9 %copy-start.1 = (f32[8,16,128]{2,1,0:T(8,128)}, f32[8,16,128]{2,1,0:T(8,128)S(1)}, u32[]{:S(2)}) copy-start(f32[8,16,128]{2,1,0:T(8,128)S(1)} %get-tuple-element.124) | copy-start | bytes 196612
  51.9 7.9 %copy-start.2 = (f32[8,16,128]{2,1,0:T(8,128)}, f32[8,16,128]{2,1,0:T(8,128)S(1)}, u32[]{:S(2)}) copy-start(f32[8,16,128]{2,1,0:T(8,128)S(1)} %get-tuple-element.125) | copy-start | bytes 196612
  54.5 20.5 %copy-start.6 = (f32[384]{0:T(512)S(1)}, f32[384]{0:T(512)}, u32[]{:S(2)}) copy-start(f32[384]{0:T(512)} %param.18) | copy-start | bytes 4612
  63.7 11.1 %all-to-all-start = ((bf16[4,4,96]{2,0,1:T(4,128)(2,1)}), bf16[4,4,96]{2,0,1:T(4,128)(2,1)S(1)}, u32[]{:S(2)}, u32[]{:S(2)}) async-start(bf16[4,4,96]{2,0,1:T(4,128)(2,1)} %copy.17), calls=%async_computation | async-start | bytes 8192 | tf_op jit(solution)/shard_map/all_to_all | solution.py:142
  69.3 64.4 %reduce-scatter.4.cloned.1.call-start = ((), (), s32[]{:S(2)}) async-start(), calls=%async_computation.3 | async-start | bytes 1114112
  155.5 8.8 %all-to-all-start.1 = ((bf16[4,4,96]{2,0,1:T(4,128)(2,1)}), bf16[4,4,96]{2,0,1:T(4,128)(2,1)S(1)}, u32[]{:S(2)}, u32[]{:S(2)}) async-start(bf16[4,4,96]{2,0,1:T(4,128)(2,1)} %copy.19), calls=%async_computation.1 | async-start | bytes 8192 | tf_op jit(solution)/shard_map/all_to_all | solution.py:165
Sparse Core Ops, SparseCore 0:
  76.9 56.7 reduce-scatter.3
where the time goes:
time: 173 us; the launch traced here: 172 us
  waiting for transfers between devices  70.5 us (41%)
  starting transfers between devices  36.6 us (21%)
  blocking collectives  19.4 us (11%)
  local copies, waits for them, and re-layouts  17 us (10%)
  between operations  15.2 us (9%)
  other arithmetic  9.79 us (6%)
  matrix products  3.65 us (2%)
    unnamed x2, waiting for transfers between devices  55.5 us
    ppermute x6, starting transfers between devices, extended(): before = lax.ppermute(last, axis, up)  20.1 us
    all_gather x1, blocking collectives, body(): lax.all_gather(modal_rounded, ('tile', 'sub', 'rep'), axis=1, tiled=True)  19.4 us
    gather x4, local copies, waits for them, and re-layouts, deep_block(): jnp.take(interior.reshape(-1), cell_index).astype(jnp.bfloat16)  10.7 us
    ppermute x6, starting transfers between devices, extended(): after = lax.ppermute(first, axis, down)  7.75 us
    all_to_all x1, waiting for transfers between devices, body(): lax.all_to_all(bucketed, 'tile', split_axis=1, concat_axis=1, tiled=True)  5.57 us
    all_to_all x1, starting transfers between devices, body(): lax.all_to_all(bucketed, 'tile', split_axis=1, concat_axis=1, tiled=True)  5.54 us
    all_to_all x1, waiting for transfers between devices, body(): lax.all_to_all(outgoing, 'tile', split_axis=1, concat_axis=1, tiled=True)  4.98 us
  transfers between devices with their start and end apart: 15, of which 6 were waited for; matrix products, arithmetic and copies ran while one was open for 5% of the time, Pallas kernels for 0%

commit v1 on v0

--- a/solution.py
+++ b/solution.py
@@ -156,7 +156,7 @@
     modal_accel, modal_state = oscillate(forces, local_frequency, local_damping, local_start)
     modal_rounded = modal_accel.astype(jnp.bfloat16)
     node_accel = lax.dot_general(
-        lax.all_gather(modal_rounded, ("tile", "sub", "rep"), axis=1, tiled=True),
+        jnp.concatenate(lax.all_gather(modal_rounded, ("tile", "sub", "rep")), axis=1),
         mode_shapes,
         (((1,), (1,)), ((), ())),
         preferred_element_type=jnp.float32,

time: 173 us -> 173 us (level)
  no operation moved by 1% of the time
where the time goes in v1:
time: 173 us; the launch traced here: 172 us
  waiting for transfers between devices  70.5 us (41%)
  starting transfers between devices  36.6 us (21%)
  blocking collectives  19.4 us (11%)
  local copies, waits for them, and re-layouts  17 us (10%)
  between operations  15.2 us (9%)
  other arithmetic  9.79 us (6%)
  matrix products  3.65 us (2%)
    unnamed x2, waiting for transfers between devices  55.5 us
    ppermute x6, starting transfers between devices, extended(): before = lax.ppermute(last, axis, up)  20.1 us
    all_gather x1, blocking collectives, body(): lax.all_gather(modal_rounded, ('tile', 'sub', 'rep'))  19.4 us
    gather x4, local copies, waits for them, and re-layouts, deep_block(): jnp.take(interior.reshape(-1), cell_index).astype(jnp.bfloat16)  10.7 us
    ppermute x6, starting transfers between devices, extended(): after = lax.ppermute(first, axis, down)  7.75 us
    all_to_all x1, waiting for transfers between devices, body(): lax.all_to_all(bucketed, 'tile', split_axis=1, concat_axis=1, tiled=True)  5.57 us
    all_to_all x1, starting transfers between devices, body(): lax.all_to_all(bucketed, 'tile', split_axis=1, concat_axis=1, tiled=True)  5.54 us
    all_to_all x1, waiting for transfers between devices, body(): lax.all_to_all(outgoing, 'tile', split_axis=1, concat_axis=1, tiled=True)  4.98 us
  transfers between devices with their start and end apart: 15, of which 6 were waited for; matrix products, arithmetic and copies ran while one was open for 5% of the time, Pallas kernels for 0%

profile of v1, /device:TPU:0, one launch (start us, length us, event | category | flops | bytes accessed | tf_op | source)
XLA Modules:
  0.0 172.1 jit_solution(18394078761567606620)
XLA Ops:
  7.2 0.9 fusion.41
  8.1 5.0 %collective-permute-start = (f32[2,4,16,128]{3,2,1,0:T(8,128)S(1)}, f32[2,4,16,128]{3,2,1,0:T(8,128)S(1)}, u32[]{:S(2)}, u32[]{:S(2)}) collective-permute-start(f32[2,4,16,128]{3,2,1,0:T(8,128)S(1)} %get-tuple-element.142), channel_id=1, source_target_pairs={{0,4},{4,8},{8,12},{1,5},{5,9},{9,13},{2,6},{6,10},{10,14},{3,7},{... | collective-permute-start | bytes 196616 | tf_op jit(solution)/shard_map/while/body/eval_jaxpr/ppermute | solution.py:19
  13.1 1.3 collective-permute-start.1
  14.4 0.8 fusion.71
  15.2 4.5 %collective-permute-start.6 = (f32[4,16,128]{2,1,0:T(8,128)S(1)}, f32[4,16,128]{2,1,0:T(8,128)S(1)}, u32[]{:S(2)}, u32[]{:S(2)}) collective-permute-start(f32[4,16,128]{2,1,0:T(8,128)S(1)} %get-tuple-element.145), channel_id=1, source_target_pairs={{0,4},{4,8},{8,12},{1,5},{5,9},{9,13},{2,6},{6,10},{10,14},{3,7},{... | collective-permute-start | bytes 98312 | tf_op jit(solution)/shard_map/ppermute | solution.py:19
  19.7 1.3 collective-permute-start.7
  21.1 0.7 reduce
  22.5 0.7 reduce.1
  23.2 0.2 fusion.1
  23.4 0.1 broadcast_multiply_fusion.1
  23.5 0.1 broadcast_multiply_fusion
  23.6 0.7 constant_dynamic-slice_fusion
  24.3 0.8 constant_dynamic-update-slice_fusion.1
  25.1 0.4 collective-permute-done.7
  25.6 3.4 %collective-permute-start.8 = (f32[16,4,128]{2,1,0:T(4,128)S(1)}, f32[16,4,128]{2,1,0:T(4,128)S(1)}, u32[]{:S(2)}, u32[]{:S(2)}) collective-permute-start(f32[16,4,128]{2,1,0:T(4,128)S(1)} %get-tuple-element.140), channel_id=1, source_target_pairs={{0,2},{1,3},{4,6},{5,7},{8,10},{9,11},{12,14},{13,15},{16,18},{17,... | collective-permute-start | bytes 98312 | tf_op jit(solution)/shard_map/ppermute | solution.py:19
  29.0 1.3 collective-permute-start.9
  30.3 0.8 pad_maximum_fusion.7
  31.1 4.5 %collective-permute-start.2 = (f32[2,16,4,128]{3,2,1,0:T(4,128)S(1)}, f32[2,16,4,128]{3,2,1,0:T(4,128)S(1)}, u32[]{:S(2)}, u32[]{:S(2)}) collective-permute-start(f32[2,16,4,128]{3,2,1,0:T(4,128)S(1)} %get-tuple-element.136), channel_id=1, source_target_pairs={{0,2},{1,3},{4,6},{5,7},{8,10},{9,11},{12,14},{13,15},{16,18},{17,... | collective-permute-start | bytes 196616 | tf_op jit(solution)/shard_map/while/body/eval_jaxpr/ppermute | solution.py:19
  35.7 1.3 collective-permute-start.3
  37.1 0.1 fusion.69
  37.2 1.3 collective-permute-start.10
  38.5 1.3 collective-permute-start.11
  39.8 2.1 %collective-permute-done.3 = f32[2,16,4,128]{3,2,1,0:T(4,128)S(1)} collective-permute-done((f32[2,16,4,128]{3,2,1,0:T(4,128)S(1)}, f32[2,16,4,128]{3,2,1,0:T(4,128)S(1)}, u32[]{:S(2)}, u32[]{:S(2)}) %collective-permute-start.3) | collective-permute-done | bytes 65568 | tf_op jit(solution)/shard_map/while/body/eval_jaxpr/ppermute | solution.py:20
  41.9 0.1 pad_maximum_fusion.1
  41.9 0.2 fusion.68
  42.1 1.3 collective-permute-start.4
  43.4 1.3 collective-permute-start.5
  44.7 0.3 pad_maximum_fusion.2
  45.1 2.0 %collective-permute-done.5 = f32[2,16,24,4]{3,2,1,0:T(8,128)S(1)} collective-permute-done((f32[2,16,24,4]{3,2,1,0:T(8,128)S(1)}, f32[2,16,24,4]{3,2,1,0:T(8,128)S(1)}, u32[]{:S(2)}, u32[]{:S(2)}) %collective-permute-start.5) | collective-permute-done | bytes 12320 | tf_op jit(solution)/shard_map/while/body/eval_jaxpr/ppermute | solution.py:20
  47.0 0.5 pad_maximum_fusion
  47.6 0.1 slice_bitcast_fusion
  47.6 0.1 fusion.61
  47.7 1.4 slice_subtract_fusion
  49.1 0.1 slice.514
  49.2 1.2 slice_subtract_fusion.1
  50.4 0.1 slice.499
  50.5 1.0 slice_subtract_fusion.2
  51.6 0.3 fusion.40
  51.9 2.5 %gather_fusion.2 = bf16[384]{0:T(512)(128)(2,1)S(1)} fusion(f32[16384]{0:T(1024)S(1)} %bitcast.49, s32[1024]{0:T(1024)S(1)} %pad_clamp_fusion), kind=kCustom, calls=%fused_computation.2.clone | custom fusion | bytes 3072 | tf_op jit(solution)/shard_map/while/body/eval_jaxpr/jit(_take)/gather | solution.py:130
  54.5 2.5 %gather_fusion.3 = bf16[384]{0:T(512)(128)(2,1)S(1)} fusion(f32[16384]{0:T(1024)S(1)} %bitcast.48, s32[1024]{0:T(1024)S(1)} %pad_clamp_fusion), kind=kCustom, calls=%fused_computation.3.clone | custom fusion | bytes 3072 | tf_op jit(solution)/shard_map/while/body/eval_jaxpr/jit(_take)/gather | solution.py:130
  57.0 2.8 %gather_fusion.1 = bf16[384]{0:T(512)(128)(2,1)S(1)} fusion(bf16[16384]{0:T(1024)(128)(2,1)S(1)} %bitcast.47, s32[1024]{0:T(1024)S(1)} %pad_clamp_fusion), kind=kCustom, calls=%fused_computation.1.clone | custom fusion | bytes 3072 | tf_op jit(solution)/shard_map/while/body/eval_jaxpr/jit(_take)/gather | solution.py:130
  59.9 2.8 %gather_fusion = bf16[384]{0:T(512)(128)(2,1)S(1)} fusion(bf16[16384]{0:T(1024)(128)(2,1)S(1)} %bitcast.46, s32[1024]{0:T(1024)S(1)} %pad_clamp_fusion), kind=kCustom, calls=%fused_computation.clone | custom fusion | bytes 3072 | tf_op jit(solution)/shard_map/while/body/eval_jaxpr/jit(_take)/gather | solution.py:130
  62.8 0.3 convolution_convert_fusion.1
  63.1 0.1 reshape.141
  63.1 0.6 copy.17
  63.7 5.5 %all-to-all-start = ((bf16[4,4,96]{2,0,1:T(4,128)(2,1)}), bf16[4,4,96]{2,0,1:T(4,128)(2,1)S(1)}, u32[]{:S(2)}, u32[]{:S(2)}) async-start(bf16[4,4,96]{2,0,1:T(4,128)(2,1)} %copy.17), calls=%async_computation | async-start | bytes 8192 | tf_op jit(solution)/shard_map/all_to_all | solution.py:142
  69.3 5.6 %all-to-all-done = bf16[4,4,96]{2,0,1:T(4,128)(2,1)S(1)} async-done(((bf16[4,4,96]{2,0,1:T(4,128)(2,1)}), bf16[4,4,96]{2,0,1:T(4,128)(2,1)S(1)}, u32[]{:S(2)}, u32[]{:S(2)}) %all-to-all-start) | async-done | bytes 3104 | tf_op jit(solution)/shard_map/all_to_all | solution.py:142
  74.9 0.1 reshape.147
  75.0 1.7 %convolution_bitcast_fusion = f32[2048,4]{1,0:T(8,128)} fusion(bf16[384,2048]{1,0:T(8,128)(2,1)S(1)} %copy-done, f32[4,384]{1,0:T(4,128)S(1)} %reshape.147, f32[384]{0:T(512)S(1)} %copy-done.6), kind=kOutput, calls=%fused_computation.6 | convolution fusion | flops 6294528 | bytes 1613312
  76.7 0.0 reduce-scatter.4.cloned.1.call-update
  76.7 0.8 fusion.64
  77.5 0.8 dynamic_slice.15
  78.3 55.4 %reduce-scatter.4.cloned.1.call-done = f32[128,4]{1,0:T(8,128)} async-done(((f32[2048,4]{1,0:T(8,128)}), f32[128,4]{1,0:T(8,128)}) %reduce-scatter.4.cloned.1.call-update) | async-done | bytes 2064
  133.7 0.9 copy.22
  134.6 0.3 while.4
  134.9 19.4 %all-gather.1 = bf16[16,4,128]{2,1,0:T(4,128)(2,1)S(1)} all-gather(bf16[1,4,128]{2,1,0:T(4,128)(2,1)S(1)} %bitcast.62), channel_id=2, replica_groups=mesh['groups'=2,'tile'=4,'sub'=2,'rep'=2] {'tile','sub','rep'}, dimensions={0}, use_global_device_ids=true | all-gather | bytes 17408 | tf_op jit(solution)/shard_map/all_gather | solution.py:159
  154.2 0.5 convolution_convert_fusion.2
  154.8 0.1 reshape.144
  154.8 0.6 copy.19
  155.5 3.2 %all-to-all-start.1 = ((bf16[4,4,96]{2,0,1:T(4,128)(2,1)}), bf16[4,4,96]{2,0,1:T(4,128)(2,1)S(1)}, u32[]{:S(2)}, u32[]{:S(2)}) async-start(bf16[4,4,96]{2,0,1:T(4,128)(2,1)} %copy.19), calls=%async_computation.1 | async-start | bytes 8192 | tf_op jit(solution)/shard_map/all_to_all | solution.py:165
  158.7 0.6 pad_maximum_fusion.9
  159.3 5.0 %all-to-all-done.1 = bf16[4,4,96]{2,0,1:T(4,128)(2,1)S(1)} async-done(((bf16[4,4,96]{2,0,1:T(4,128)(2,1)}), bf16[4,4,96]{2,0,1:T(4,128)(2,1)S(1)}, u32[]{:S(2)}, u32[]{:S(2)}) %all-to-all-start.1) | async-done | bytes 3104 | tf_op jit(solution)/shard_map/all_to_all | solution.py:165
  164.3 0.1 reshape.145
  164.4 0.9 fusion.2
  (53 shorter events, 0.5 us)
Async XLA Ops:
  7.2 67.8 %copy-start = (bf16[384,2048]{1,0:T(8,128)(2,1)S(1)}, bf16[384,2048]{1,0:T(8,128)(2,1)}, u32[]{:S(2)}) copy-start(bf16[384,2048]{1,0:T(8,128)(2,1)} %param.19) | copy-start | bytes 4718596
  7.2 34.7 %copy-start.3 = (f32[8,16,128]{2,1,0:T(8,128)S(1)}, f32[8,16,128]{2,1,0:T(8,128)}, u32[]{:S(2)}) copy-start(f32[8,16,128]{2,1,0:T(8,128)} %param.15) | copy-start | bytes 196612
  7.2 34.7 %copy-start.4 = (f32[8,16,128]{2,1,0:T(8,128)S(1)}, f32[8,16,128]{2,1,0:T(8,128)}, u32[]{:S(2)}) copy-start(f32[8,16,128]{2,1,0:T(8,128)} %param.16) | copy-start | bytes 196612
  8.1 22.1 %collective-permute-start = (f32[2,4,16,128]{3,2,1,0:T(8,128)S(1)}, f32[2,4,16,128]{3,2,1,0:T(8,128)S(1)}, u32[]{:S(2)}, u32[]{:S(2)}) collective-permute-start(f32[2,4,16,128]{3,2,1,0:T(8,128)S(1)} %get-tuple-element.142), channel_id=1, source_target_pairs={{0,4},{4,8},{8,12},{1,5},{5,9},{9,13},{2,6},{6,10},{10,14},{3,7},{... | collective-permute-start | bytes 196616 | tf_op jit(solution)/shard_map/while/body/eval_jaxpr/ppermute | solution.py:19
  13.1 17.2 %collective-permute-start.1 = (f32[2,4,16,128]{3,2,1,0:T(8,128)S(1)}, f32[2,4,16,128]{3,2,1,0:T(8,128)S(1)}, u32[]{:S(2)}, u32[]{:S(2)}) collective-permute-start(f32[2,4,16,128]{3,2,1,0:T(8,128)S(1)} %get-tuple-element.143), channel_id=1, source_target_pairs={{4,0},{8,4},{12,8},{5,1},{9,5},{13,9},{6,2},{10,6},{14,10},{7,3},{... | collective-permute-start | bytes 196616 | tf_op jit(solution)/shard_map/while/body/eval_jaxpr/ppermute | solution.py:20
  15.2 9.1 %collective-permute-start.6 = (f32[4,16,128]{2,1,0:T(8,128)S(1)}, f32[4,16,128]{2,1,0:T(8,128)S(1)}, u32[]{:S(2)}, u32[]{:S(2)}) collective-permute-start(f32[4,16,128]{2,1,0:T(8,128)S(1)} %get-tuple-element.145), channel_id=1, source_target_pairs={{0,4},{4,8},{8,12},{1,5},{5,9},{9,13},{2,6},{6,10},{10,14},{3,7},{... | collective-permute-start | bytes 98312 | tf_op jit(solution)/shard_map/ppermute | solution.py:19
  19.7 5.8 %collective-permute-start.7 = (f32[4,16,128]{2,1,0:T(8,128)S(1)}, f32[4,16,128]{2,1,0:T(8,128)S(1)}, u32[]{:S(2)}, u32[]{:S(2)}) collective-permute-start(f32[4,16,128]{2,1,0:T(8,128)S(1)} %get-tuple-element.144), channel_id=1, source_target_pairs={{4,0},{8,4},{12,8},{5,1},{9,5},{13,9},{6,2},{10,6},{14,10},{7,3},{... | collective-permute-start | bytes 98312 | tf_op jit(solution)/shard_map/ppermute | solution.py:20
  25.6 11.4 %collective-permute-start.8 = (f32[16,4,128]{2,1,0:T(4,128)S(1)}, f32[16,4,128]{2,1,0:T(4,128)S(1)}, u32[]{:S(2)}, u32[]{:S(2)}) collective-permute-start(f32[16,4,128]{2,1,0:T(4,128)S(1)} %get-tuple-element.140), channel_id=1, source_target_pairs={{0,2},{1,3},{4,6},{5,7},{8,10},{9,11},{12,14},{13,15},{16,18},{17,... | collective-permute-start | bytes 98312 | tf_op jit(solution)/shard_map/ppermute | solution.py:19
  29.0 8.0 %collective-permute-start.9 = (f32[16,4,128]{2,1,0:T(4,128)S(1)}, f32[16,4,128]{2,1,0:T(4,128)S(1)}, u32[]{:S(2)}, u32[]{:S(2)}) collective-permute-start(f32[16,4,128]{2,1,0:T(4,128)S(1)} %get-tuple-element.141), channel_id=1, source_target_pairs={{2,0},{3,1},{6,4},{7,5},{10,8},{11,9},{14,12},{15,13},{18,16},{19,... | collective-permute-start | bytes 98312 | tf_op jit(solution)/shard_map/ppermute | solution.py:20
  31.1 8.6 %collective-permute-start.2 = (f32[2,16,4,128]{3,2,1,0:T(4,128)S(1)}, f32[2,16,4,128]{3,2,1,0:T(4,128)S(1)}, u32[]{:S(2)}, u32[]{:S(2)}) collective-permute-start(f32[2,16,4,128]{3,2,1,0:T(4,128)S(1)} %get-tuple-element.136), channel_id=1, source_target_pairs={{0,2},{1,3},{4,6},{5,7},{8,10},{9,11},{12,14},{13,15},{16,18},{17,... | collective-permute-start | bytes 196616 | tf_op jit(solution)/shard_map/while/body/eval_jaxpr/ppermute | solution.py:19
  35.7 6.2 %collective-permute-start.3 = (f32[2,16,4,128]{3,2,1,0:T(4,128)S(1)}, f32[2,16,4,128]{3,2,1,0:T(4,128)S(1)}, u32[]{:S(2)}, u32[]{:S(2)}) collective-permute-start(f32[2,16,4,128]{3,2,1,0:T(4,128)S(1)} %get-tuple-element.137), channel_id=1, source_target_pairs={{2,0},{3,1},{6,4},{7,5},{10,8},{11,9},{14,12},{15,13},{18,16},{19,... | collective-permute-start | bytes 196616 | tf_op jit(solution)/shard_map/while/body/eval_jaxpr/ppermute | solution.py:20
  37.2 7.6 %collective-permute-start.10 = (f32[16,24,4]{2,1,0:T(8,128)S(1)}, f32[16,24,4]{2,1,0:T(8,128)S(1)}, u32[]{:S(2)}, u32[]{:S(2)}) collective-permute-start(f32[16,24,4]{2,1,0:T(8,128)S(1)} %get-tuple-element.138), channel_id=1, source_target_pairs={{0,1},{2,3},{4,5},{6,7},{8,9},{10,11},{12,13},{14,15},{16,17},{18,... | collective-permute-start | bytes 18440 | tf_op jit(solution)/shard_map/ppermute | solution.py:19
  38.5 6.3 %collective-permute-start.11 = (f32[16,24,4]{2,1,0:T(8,128)S(1)}, f32[16,24,4]{2,1,0:T(8,128)S(1)}, u32[]{:S(2)}, u32[]{:S(2)}) collective-permute-start(f32[16,24,4]{2,1,0:T(8,128)S(1)} %get-tuple-element.139), channel_id=1, source_target_pairs={{1,0},{3,2},{5,4},{7,6},{9,8},{11,10},{13,12},{15,14},{17,16},{19,... | collective-permute-start | bytes 18440 | tf_op jit(solution)/shard_map/ppermute | solution.py:20
  42.1 2.9 %collective-permute-start.4 = (f32[2,16,24,4]{3,2,1,0:T(8,128)S(1)}, f32[2,16,24,4]{3,2,1,0:T(8,128)S(1)}, u32[]{:S(2)}, u32[]{:S(2)}) collective-permute-start(f32[2,16,24,4]{3,2,1,0:T(8,128)S(1)} %get-tuple-element.134), channel_id=1, source_target_pairs={{0,1},{2,3},{4,5},{6,7},{8,9},{10,11},{12,13},{14,15},{16,17},{18,... | collective-permute-start | bytes 36872 | tf_op jit(solution)/shard_map/while/body/eval_jaxpr/ppermute | solution.py:19
  43.4 3.6 %collective-permute-start.5 = (f32[2,16,24,4]{3,2,1,0:T(8,128)S(1)}, f32[2,16,24,4]{3,2,1,0:T(8,128)S(1)}, u32[]{:S(2)}, u32[]{:S(2)}) collective-permute-start(f32[2,16,24,4]{3,2,1,0:T(8,128)S(1)} %get-tuple-element.135), channel_id=1, source_target_pairs={{1,0},{3,2},{5,4},{7,6},{9,8},{11,10},{13,12},{15,14},{17,16},{19,... | collective-permute-start | bytes 36872 | tf_op jit(solution)/shard_map/while/body/eval_jaxpr/ppermute | solution.py:20
  50.5 1.1 copy-start.5
  51.9 7.9 %copy-start.1 = (f32[8,16,128]{2,1,0:T(8,128)}, f32[8,16,128]{2,1,0:T(8,128)S(1)}, u32[]{:S(2)}) copy-start(f32[8,16,128]{2,1,0:T(8,128)S(1)} %get-tuple-element.124) | copy-start | bytes 196612
  51.9 7.9 %copy-start.2 = (f32[8,16,128]{2,1,0:T(8,128)}, f32[8,16,128]{2,1,0:T(8,128)S(1)}, u32[]{:S(2)}) copy-start(f32[8,16,128]{2,1,0:T(8,128)S(1)} %get-tuple-element.125) | copy-start | bytes 196612
  54.5 20.5 %copy-start.6 = (f32[384]{0:T(512)S(1)}, f32[384]{0:T(512)}, u32[]{:S(2)}) copy-start(f32[384]{0:T(512)} %param.18) | copy-start | bytes 4612
  63.7 11.1 %all-to-all-start = ((bf16[4,4,96]{2,0,1:T(4,128)(2,1)}), bf16[4,4,96]{2,0,1:T(4,128)(2,1)S(1)}, u32[]{:S(2)}, u32[]{:S(2)}) async-start(bf16[4,4,96]{2,0,1:T(4,128)(2,1)} %copy.17), calls=%async_computation | async-start | bytes 8192 | tf_op jit(solution)/shard_map/all_to_all | solution.py:142
  69.3 64.4 %reduce-scatter.4.cloned.1.call-start = ((), (), s32[]{:S(2)}) async-start(), calls=%async_computation.3 | async-start | bytes 1114112
  155.5 8.8 %all-to-all-start.1 = ((bf16[4,4,96]{2,0,1:T(4,128)(2,1)}), bf16[4,4,96]{2,0,1:T(4,128)(2,1)S(1)}, u32[]{:S(2)}, u32[]{:S(2)}) async-start(bf16[4,4,96]{2,0,1:T(4,128)(2,1)} %copy.19), calls=%async_computation.1 | async-start | bytes 8192 | tf_op jit(solution)/shard_map/all_to_all | solution.py:165
Sparse Core Ops, SparseCore 0:
  76.9 56.7 reduce-scatter.3
